TPU v7x, 256 devices: a whole 4x4x8 slice. The times are simulated.
256 devices in a mesh: dp: 32 (over x, z), rows: 8 (over y, core).
Axes of the slice: x: 4, y: 4, z: 8, core: 2. Of those that a mesh axis runs over, the one named last changes fastest.
Arguments:
- activations: bfloat16 [65536, 8192], P('dp', 'rows'), may hold values from -6 to 6
- key_grads: bfloat16 [65536, 1024], P('dp'), may hold values from -0.125 to 0.125
- momentum: float32 [32, 8192, 1024], P('dp', 'rows'), may hold values from -6 to 6
- basis: float32 [1024, 128], replicated, may hold values from -0.1875 to 0.1875
Outputs:
- new_momentum: float32 [32, 8192, 1024], P('dp', 'rows')
- new_basis: float32 [1024, 128], P('rows')
- update: bfloat16 [8192, 1024], P(('rows', 'dp'))
All inputs are finite; a program needn't handle non-finite values.
Results may differ from a plain program's by a relative error of at most 0.0015.
Values sent between devices are 32-bit elements; how exact they have to be, the bound alone decides.
A program may use at most 64 MiB of HBM per device.

v0:
```python
import math
import jax
import jax.numpy as jnp
from jax import lax
from jax.sharding import PartitionSpec as P

D = 8192
KV = 1024
RANK = 128


def body(activations, key_grads, momentum, basis):
    high = lax.Precision.HIGHEST
    n_dp = lax.axis_size("dp")
    n_rows = lax.axis_size("rows")
    grad = lax.dot_general(
        activations, key_grads, (((0,), (0,)), ((), ())), preferred_element_type=jnp.float32
    )
    blended = momentum[0] + grad
    local_rows = blended.shape[0]
    own_count = local_rows // n_dp
    sketch = jnp.dot(blended, basis, precision=high)
    total = lax.psum(sketch, "dp") / n_dp
    gram = lax.psum(jnp.dot(total.T, total, precision=high), "rows")
    lower = jnp.linalg.cholesky(gram)
    ortho = lax.linalg.triangular_solve(lower, total, left_side=False, lower=True, transpose_a=True)
    own_rows = lax.dynamic_slice_in_dim(ortho, lax.axis_index("dp") * own_count, own_count, 0)
    partial_coeff = lax.dot_general(
        blended, ortho, (((0,), (0,)), ((), ())), precision=high, preferred_element_type=jnp.float32
    )
    row_total = lax.psum(partial_coeff, "rows")
    coeff = lax.psum(row_total, "dp") / n_dp
    feedback = lax.dot_general(
        ortho, coeff, (((1,), (1,)), ((), ())), precision=high, preferred_element_type=jnp.float32
    )
    new_momentum = (blended - 0.2 * feedback)[None]
    col_norm = jnp.sqrt(jnp.sum(coeff * coeff, axis=0) + 1e-06)
    normed = coeff / col_norm
    basis_rows = normed.shape[0] // n_rows
    new_basis = lax.dynamic_slice_in_dim(normed, lax.axis_index("rows") * basis_rows, basis_rows, 0)
    scale = math.sqrt(D * KV / RANK)
    update = scale * lax.dot_general(
        own_rows,
        normed,
        (((1,), (1,)), ((), ())),
        precision=high,
        preferred_element_type=jnp.float32,
    )
    return (new_momentum, new_basis, update.astype(jnp.bfloat16))


def solution(mesh):
    in_specs = (P("dp", "rows"), P("dp", None), P("dp", "rows", None), P())
    out_specs = (P("dp", "rows", None), P("rows", None), P(("rows", "dp"), None))
    return jax.shard_map(body, mesh=mesh, in_specs=in_specs, out_specs=out_specs, check_vma=False)
```

profile of v0, /device:TPU:8, one launch (start us, length us, event | category | flops | bytes accessed | tf_op | source)
XLA Modules:
  0.0 509.6 jit_solution(2089258059151605562)
XLA Ops:
  7.2 0.0 copy-start
  7.2 0.0 all-reduce.5.cloned.1.call-start
  7.2 9.3 %bitcast_add_fusion = f32[1024,1024]{1,0:T(8,128)S(1)} fusion(f32[1,1024,1024]{2,1,0:T(8,128)} %param.6, bf16[2048,1024]{1,0:T(8,128)(2,1)} %param.4, bf16[2048,1024]{1,0:T(8,128)(2,1)} %param.5), kind=kOutput, calls=%fused_computation | convolution fusion | flops 4296015872 | bytes 16777216 | tf_op jit(solution)/shard_map/dot_general | solution.py:16
  16.5 0.0 copy-start.1
  16.5 2.0 copy-done.1
  18.5 0.0 copy-done
  18.5 4.2 fusion.17
  22.7 0.0 all-reduce.5.cloned.1.call-update
  22.8 0.0 all-reduce.7.cloned.1.call-start
  22.8 151.7 %all-reduce.5.cloned.1.call-done = f32[1024,128]{1,0:T(8,128)} async-done(((f32[1024,128]{1,0:T(8,128)}), f32[1024,128]{1,0:T(8,128)}) %all-reduce.5.cloned.1.call-update) | async-done | bytes 524304 | tf_op jit(solution)/shard_map/psum | solution.py:23
  174.5 2.8 fusion.3
  177.4 0.0 all-reduce.7.cloned.1.call-update
  177.4 0.2 all-reduce.9.cloned.1.call-start
  177.6 59.7 %all-reduce.7.cloned.1.call-done = f32[128,128]{0,1:T(8,128)} async-done(((f32[128,128]{0,1:T(8,128)}), f32[128,128]{0,1:T(8,128)}) %all-reduce.7.cloned.1.call-update) | async-done | bytes 65552 | tf_op jit(solution)/shard_map/psum | solution.py:24
  237.3 0.9 copy.8
  238.3 0.9 fusion.11
  239.1 11.7 %cholesky.16 = f32[128,128]{1,0:T(8,128)S(1)} custom-call(f32[128,128]{1,0:T(8,128)S(1)} %fusion.11), custom_call_target="Cholesky" | custom-call | tf_op jit(solution)/shard_map/jit(cholesky)/cholesky | solution.py:25
  250.9 0.6 compare_reduce_fusion
  251.5 0.7 fusion.9
  252.2 9.8 %custom-call.6 = f32[1,128,128]{1,2,0:T(8,128)S(1)} custom-call(f32[1,128,128]{2,1,0:T(8,128)S(1)} %fusion.9), custom_call_target="InvertDiagBlocksLowerTriangular" | custom-call | tf_op jit(solution)/shard_map/triangular_solve | solution.py:26
  262.0 1.6 fusion.1
  263.6 9.9 %fusion.18 = f32[1024,128]{1,0:T(8,128)} fusion(f32[1024,1024]{1,0:T(8,128)} %copy-done.1, f32[1024,128]{1,0:T(8,128)S(1)} %fusion.1), kind=kOutput, calls=%fused_computation.31 | convolution fusion | flops 1610612736 | bytes 5242880 | tf_op jit(solution)/shard_map/dot_general | solution.py:28
  273.5 0.0 all-reduce.9.cloned.1.call-update
  273.5 0.0 all-reduce.11.cloned.1.call-start
  273.5 65.3 %all-reduce.9.cloned.1.call-done = f32[1024,128]{1,0:T(8,128)} async-done(((f32[1024,128]{1,0:T(8,128)}), f32[1024,128]{1,0:T(8,128)}) %all-reduce.9.cloned.1.call-update) | async-done | bytes 524304 | tf_op jit(solution)/shard_map/psum | solution.py:31
  338.8 0.0 all-reduce.11.cloned.1.call-update
  338.8 153.3 %all-reduce.11.cloned.1.call-done = f32[1024,128]{1,0:T(8,128)} async-done(((f32[1024,128]{1,0:T(8,128)}), f32[1024,128]{1,0:T(8,128)}) %all-reduce.11.cloned.1.call-update) | async-done | bytes 524304 | tf_op jit(solution)/shard_map/psum | solution.py:32
  492.2 1.2 multiply_reduce_fusion
  493.4 1.1 multiply_divide_fusion
  494.5 0.6 constant_dynamic-slice_fusion
  495.1 1.2 fusion
  496.4 6.7 %subtract_bitcast_fusion = f32[1,1024,1024]{2,1,0:T(8,128)} fusion(f32[1024,1024]{1,0:T(8,128)} %copy-done.1, f32[1024,128]{1,0:T(8,128)S(1)} %fusion.1, f32[1024,128]{1,0:T(8,128)} %all-reduce.11.cloned.1.call-done), kind=kOutput, calls=%fused_computation.1 | convolution fusion | flops 1612840960 | bytes 9437184 | tf_op jit(solution)/shard_map/dot_general | solution.py:33
  (2 shorter events, 0.0 us)
Async XLA Ops:
  7.2 11.3 %copy-start = (f32[1024,128]{1,0:T(8,128)S(1)}, f32[1024,128]{1,0:T(8,128)}, u32[]{:S(2)}) copy-start(f32[1024,128]{1,0:T(8,128)} %param.7) | copy-start | bytes 1572868
  7.2 167.4 %all-reduce.5.cloned.1.call-start = ((), (), s32[]{:S(2)}) async-start(), calls=%async_computation | async-start | bytes 1048576 | tf_op jit(solution)/shard_map/psum | solution.py:23
  16.5 2.0 copy-start.1
  22.8 214.5 %all-reduce.7.cloned.1.call-start = ((), (), s32[]{:S(2)}) async-start(), calls=%async_computation.1 | async-start | bytes 131072 | tf_op jit(solution)/shard_map/psum | solution.py:24
  177.4 161.4 %all-reduce.9.cloned.1.call-start = ((), (), s32[]{:S(2)}) async-start(), calls=%async_computation.2 | async-start | bytes 1048576 | tf_op jit(solution)/shard_map/psum | solution.py:31
  273.5 218.7 %all-reduce.11.cloned.1.call-start = ((), (), s32[]{:S(2)}) async-start(), calls=%async_computation.3 | async-start | bytes 1048576 | tf_op jit(solution)/shard_map/psum | solution.py:32
Sparse Core Ops, SparseCore 0:
  22.9 151.5 all-reduce.4
  177.5 59.7 all-reduce.6
  273.6 65.1 all-reduce.8
  342.1 150.0 all-reduce.10
where the time goes:
time: 510 us
  waiting for transfers between devices  430 us (84%)
  matrix products  35.8 us (7%)
  other arithmetic  26 us (5%)
  between operations  13.8 us (3%)
    psum x1, waiting for transfers between devices, body(): coeff = lax.psum(row_total, 'dp') / n_dp  153 us
    psum x1, waiting for transfers between devices, body(): total = lax.psum(sketch, 'dp') / n_dp  152 us
    psum x1, waiting for transfers between devices, body(): row_total = lax.psum(partial_coeff, 'rows')  65.3 us
    psum x1, waiting for transfers between devices, body(): gram = lax.psum(jnp.dot(total.T, total, precision=high), 'rows')  59.7 us
    another operation x3, other arithmetic, body(): lower = jnp.linalg.cholesky(gram)  12.4 us
    another operation x2, other arithmetic, body(): lax.linalg.triangular_solve(lower, total, left_side=False, lower=True, tr...  10.5 us
  transfers between devices with their start and end apart: 4, of which 4 were waited for; matrix products, arithmetic and copies ran while one was open for 0% of the time, Pallas kernels for 0%

commit v1 on v0

--- a/solution.py
+++ b/solution.py
@@ -28,7 +28,11 @@
     partial_coeff = lax.dot_general(
         blended, ortho, (((0,), (0,)), ((), ())), precision=high, preferred_element_type=jnp.float32
     )
-    row_total = lax.psum(partial_coeff, "rows")
+    row_total = partial_coeff
+    for hop in (1, 2, 4):
+        row_total = row_total + lax.ppermute(
+            row_total, "rows", [(dev, dev ^ hop) for dev in range(8)]
+        )
     coeff = lax.psum(row_total, "dp") / n_dp
     feedback = lax.dot_general(
         ortho, coeff, (((1,), (1,)), ((), ())), precision=high, preferred_element_type=jnp.float32

time: 510 us -> 472 us (0.925)
  waiting for transfers between devices: 430 us -> 388 us
    psum x1 -> x0, waiting for transfers between devices: 65.3 us -> none  [body(): row_total = lax.psum(partial_coeff, 'rows')]
    ppermute x0 -> x3, waiting for transfers between devices: none -> 27.4 us  [body(): lax.ppermute(row_total, 'rows', [(dev, dev ^ hop) for dev in range(8)])]
  transfers between devices with their start and end apart: 4 -> 6, of which waited for: 4 -> 6; matrix products, arithmetic and copies ran while one was open for 0% -> 0% of each run, Pallas kernels for 0% -> 0%
where the time goes in v1:
time: 472 us
  waiting for transfers between devices  388 us (82%)
  matrix products  34.4 us (7%)
  other arithmetic  27 us (6%)
  between operations  13.8 us (3%)
  starting transfers between devices  5.17 us (1%)
    psum x1, waiting for transfers between devices, body(): total = lax.psum(sketch, 'dp') / n_dp  152 us
    psum x1, waiting for transfers between devices, body(): coeff = lax.psum(row_total, 'dp') / n_dp  149 us
    psum x1, waiting for transfers between devices, body(): gram = lax.psum(jnp.dot(total.T, total, precision=high), 'rows')  59.7 us
    ppermute x3, waiting for transfers between devices, body(): lax.ppermute(row_total, 'rows', [(dev, dev ^ hop) for dev in range(8)])  27.4 us
    another operation x3, other arithmetic, body(): lower = jnp.linalg.cholesky(gram)  12.4 us
    another operation x2, other arithmetic, body(): lax.linalg.triangular_solve(lower, total, left_side=False, lower=True, tr...  10.5 us
  transfers between devices with their start and end apart: 6, of which 6 were waited for; matrix products, arithmetic and copies ran while one was open for 0% of the time, Pallas kernels for 0%

profile of v1, /device:TPU:8, one launch (start us, length us, event | category | flops | bytes accessed | tf_op | source)
XLA Modules:
  0.0 472.0 jit_solution(6530372520997099610)
XLA Ops:
  7.2 0.0 copy-start
  7.2 0.0 all-reduce.4.cloned.1.call-start
  7.2 9.3 %bitcast_add_fusion = f32[1024,1024]{1,0:T(8,128)S(1)} fusion(f32[1,1024,1024]{2,1,0:T(8,128)} %param.6, bf16[2048,1024]{1,0:T(8,128)(2,1)} %param.4, bf16[2048,1024]{1,0:T(8,128)(2,1)} %param.5), kind=kOutput, calls=%fused_computation | convolution fusion | flops 4296015872 | bytes 16777216 | tf_op jit(solution)/shard_map/dot_general | solution.py:16
  16.5 0.0 copy-start.1
  16.5 2.0 copy-done.1
  18.5 0.0 copy-done
  18.5 4.2 fusion.17
  22.7 0.0 all-reduce.4.cloned.1.call-update
  22.8 0.0 all-reduce.6.cloned.1.call-start
  22.8 151.7 %all-reduce.4.cloned.1.call-done = f32[1024,128]{1,0:T(8,128)} async-done(((f32[1024,128]{1,0:T(8,128)}), f32[1024,128]{1,0:T(8,128)}) %all-reduce.4.cloned.1.call-update) | async-done | bytes 524304 | tf_op jit(solution)/shard_map/psum | solution.py:23
  174.5 2.8 fusion.3
  177.4 0.0 all-reduce.6.cloned.1.call-update
  177.4 0.2 all-reduce.8.cloned.1.call-start
  177.6 59.7 %all-reduce.6.cloned.1.call-done = f32[128,128]{0,1:T(8,128)} async-done(((f32[128,128]{0,1:T(8,128)}), f32[128,128]{0,1:T(8,128)}) %all-reduce.6.cloned.1.call-update) | async-done | bytes 65552 | tf_op jit(solution)/shard_map/psum | solution.py:24
  237.3 0.9 copy.8
  238.3 0.9 fusion.11
  239.1 11.7 %cholesky.16 = f32[128,128]{1,0:T(8,128)S(1)} custom-call(f32[128,128]{1,0:T(8,128)S(1)} %fusion.11), custom_call_target="Cholesky" | custom-call | tf_op jit(solution)/shard_map/jit(cholesky)/cholesky | solution.py:25
  250.9 0.6 compare_reduce_fusion
  251.5 0.7 fusion.9
  252.2 9.8 %custom-call.6 = f32[1,128,128]{1,2,0:T(8,128)S(1)} custom-call(f32[1,128,128]{2,1,0:T(8,128)S(1)} %fusion.9), custom_call_target="InvertDiagBlocksLowerTriangular" | custom-call | tf_op jit(solution)/shard_map/triangular_solve | solution.py:26
  262.0 1.6 fusion.1
  263.6 8.5 %fusion.18 = f32[1024,128]{1,0:T(8,128)S(1)} fusion(f32[1024,1024]{1,0:T(8,128)} %copy-done.1, f32[1024,128]{1,0:T(8,128)S(1)} %fusion.1), kind=kOutput, calls=%fused_computation.31 | convolution fusion | flops 1610612736 | bytes 5242880 | tf_op jit(solution)/shard_map/dot_general | solution.py:28
  272.1 0.1 collective-permute-start
  272.2 1.9 collective-permute-done
  274.1 0.1 add.47
  274.1 2.9 collective-permute-start.1
  277.0 12.2 %collective-permute-done.1 = f32[1024,128]{1,0:T(8,128)S(1)} collective-permute-done((f32[1024,128]{1,0:T(8,128)S(1)}, f32[1024,128]{1,0:T(8,128)S(1)}, u32[]{:S(2)}, u32[]{:S(2)}) %collective-permute-start.1) | collective-permute-done | bytes 524320 | tf_op jit(solution)/shard_map/ppermute | solution.py:33
  289.2 0.1 add.48
  289.3 1.9 collective-permute-start.2
  291.2 13.3 %collective-permute-done.2 = f32[1024,128]{1,0:T(8,128)S(1)} collective-permute-done((f32[1024,128]{1,0:T(8,128)S(1)}, f32[1024,128]{1,0:T(8,128)S(1)}, u32[]{:S(2)}, u32[]{:S(2)}) %collective-permute-start.2) | collective-permute-done | bytes 524320 | tf_op jit(solution)/shard_map/ppermute | solution.py:33
  304.5 0.9 add.49
  305.4 0.0 all-reduce.8.cloned.1.call-update
  305.4 149.2 %all-reduce.8.cloned.1.call-done = f32[1024,128]{1,0:T(8,128)} async-done(((f32[1024,128]{1,0:T(8,128)}), f32[1024,128]{1,0:T(8,128)}) %all-reduce.8.cloned.1.call-update) | async-done | bytes 524304 | tf_op jit(solution)/shard_map/psum | solution.py:36
  454.6 1.2 multiply_reduce_fusion
  455.8 1.1 multiply_divide_fusion
  456.9 0.6 constant_dynamic-slice_fusion
  457.5 1.2 fusion
  458.7 6.7 %subtract_bitcast_fusion = f32[1,1024,1024]{2,1,0:T(8,128)} fusion(f32[1024,1024]{1,0:T(8,128)} %copy-done.1, f32[1024,128]{1,0:T(8,128)S(1)} %fusion.1, f32[1024,128]{1,0:T(8,128)} %all-reduce.8.cloned.1.call-done), kind=kOutput, calls=%fused_computation.1 | convolution fusion | flops 1612840960 | bytes 9437184 | tf_op jit(solution)/shard_map/dot_general | solution.py:37
  (2 shorter events, 0.0 us)
Async XLA Ops:
  7.2 11.3 %copy-start = (f32[1024,128]{1,0:T(8,128)S(1)}, f32[1024,128]{1,0:T(8,128)}, u32[]{:S(2)}) copy-start(f32[1024,128]{1,0:T(8,128)} %param.7) | copy-start | bytes 1572868
  7.2 167.4 %all-reduce.4.cloned.1.call-start = ((), (), s32[]{:S(2)}) async-start(), calls=%async_computation | async-start | bytes 1048576 | tf_op jit(solution)/shard_map/psum | solution.py:23
  16.5 2.0 copy-start.1
  22.8 214.5 %all-reduce.6.cloned.1.call-start = ((), (), s32[]{:S(2)}) async-start(), calls=%async_computation.1 | async-start | bytes 131072 | tf_op jit(solution)/shard_map/psum | solution.py:24
  177.4 277.2 %all-reduce.8.cloned.1.call-start = ((), (), s32[]{:S(2)}) async-start(), calls=%async_computation.2 | async-start | bytes 1048576 | tf_op jit(solution)/shard_map/psum | solution.py:36
  272.1 2.0 collective-permute-start
  274.1 15.1 %collective-permute-start.1 = (f32[1024,128]{1,0:T(8,128)S(1)}, f32[1024,128]{1,0:T(8,128)S(1)}, u32[]{:S(2)}, u32[]{:S(2)}) collective-permute-start(f32[1024,128]{1,0:T(8,128)S(1)} %add.47), channel_id=1, source_target_pairs={{0,2},{1,3},{2,0},{3,1},{4,6},{5,7},{6,4},{7,5},{8,10},{9,11},{10,... | collective-permute-start | bytes 1572872 | tf_op jit(solution)/shard_map/ppermute | solution.py:33
  289.3 15.2 %collective-permute-start.2 = (f32[1024,128]{1,0:T(8,128)S(1)}, f32[1024,128]{1,0:T(8,128)S(1)}, u32[]{:S(2)}, u32[]{:S(2)}) collective-permute-start(f32[1024,128]{1,0:T(8,128)S(1)} %add.48), channel_id=1, source_target_pairs={{0,4},{1,5},{2,6},{3,7},{4,0},{5,1},{6,2},{7,3},{8,12},{9,13},{10,... | collective-permute-start | bytes 1572872 | tf_op jit(solution)/shard_map/ppermute | solution.py:33
Sparse Core Ops, SparseCore 0:
  22.9 151.5 all-reduce.3
  177.5 59.7 all-reduce.5
  305.5 149.0 all-reduce.7
